TPU v7x, 128 devices: a whole 4x4x4 slice. The times are simulated.
128 devices in a mesh: pair: 16 (over y_hi, z, core), rows: 8 (over y_lo, x).
Axes of the slice: x: 4, y: 4 (y_hi: 2, y_lo: 2; y = y_hi * 2 + y_lo), z: 4, core: 2. Of those that a mesh axis runs over, the one named last changes fastest.
Arguments:
- matrix: float32 [4096, 16384], P(('rows', 'pair')), may hold values from -6 to 6
- plan: int32 [32], replicated, may hold values from 0 to 31, each once
Outputs:
- rotated: float32 [4096, 16384], P('rows', 'pair')
Inputs may be any that keep to these rules, and one draw needn't show every extreme that they name: `plan`: each block number appears once.
All inputs are finite; a program needn't handle non-finite values.
Results may differ from a plain program's by a relative error of at most 0.0003.
Values sent between devices are 32-bit elements; how exact they have to be, the bound alone decides.
A program may use at most 64 MiB of HBM per device.

v0:
```python
import functools

import jax
import jax.numpy as jnp
from jax import lax
from jax.experimental import pallas as pl
from jax.experimental.pallas import tpu as pltpu
from jax.sharding import PartitionSpec as P

MESH = pl.DeviceIdType.MESH

BLK = 512
STEPS = 2


epsilon = 1e-06
high = lax.Precision.HIGHEST
fast = lax.Precision.HIGH


def shifted(v, axis, count, by):
    return lax.ppermute(v, axis, [(i, (i + by) % count) for i in range(count)])


def scatter_sum(v, axis, count):
    me = lax.axis_index(axis)
    chunks = v.reshape(count, v.shape[0] // count, *v.shape[1:])
    total = lax.dynamic_index_in_dim(chunks, me, keepdims=False)
    for by in range(1, count):
        piece = lax.dynamic_index_in_dim(chunks, (me + by) % count, keepdims=False)
        total = total + shifted(piece, axis, count, by)
    return total


def gather_all(v, axis, count):
    me = lax.axis_index(axis)
    out = jnp.zeros((count,) + v.shape, v.dtype)
    out = lax.dynamic_update_index_in_dim(out, v, me, 0)
    for by in range(1, count):
        out = lax.dynamic_update_index_in_dim(out, shifted(v, axis, count, by), (me - by) % count, 0)
    return out.reshape(count * v.shape[0], *v.shape[1:])


def rows_sum_kernel(
    outer, inner, payload, out, received, acc, halves, own, gathered, send_sem, recv_sem, y_send, y_recv, ag_send, ag_recv
):
    pair = lax.axis_index("pair")
    me_y = lax.axis_index("ylo")
    me_x = lax.axis_index("x")
    chunk = payload.shape[0] // inner
    half = chunk // outer
    partner = (me_y + 1) % outer

    barrier = pltpu.get_barrier_semaphore()
    for by in range(1, inner):
        pl.semaphore_signal(barrier, inc=1, device_id=(pair, me_y, (me_x + by) % inner), device_id_type=MESH)
    pl.semaphore_signal(barrier, inc=1, device_id=(pair, partner, me_x), device_id_type=MESH)
    pl.semaphore_wait(barrier, inner)

    copies = []
    for by in range(1, inner):
        target = (me_x + by) % inner
        copy = pltpu.make_async_remote_copy(
            src_ref=payload.at[pl.ds(pl.multiple_of(target * chunk, 8), chunk)],
            dst_ref=received.at[by - 1],
            send_sem=send_sem.at[by - 1],
            recv_sem=recv_sem.at[by - 1],
            device_id=(pair, me_y, target),
            device_id_type=MESH,
        )
        copy.start()
        copies.append(copy)
    for copy in copies:
        copy.wait()
    total = payload[pl.ds(pl.multiple_of(me_x * chunk, 8), chunk), :]
    for by in range(1, inner):
        total = total + received[by - 1]
    acc[...] = total

    copy = pltpu.make_async_remote_copy(
        src_ref=acc.at[pl.ds(pl.multiple_of(partner * half, 8), half)],
        dst_ref=halves.at[0],
        send_sem=y_send.at[0],
        recv_sem=y_recv.at[0],
        device_id=(pair, partner, me_x),
        device_id_type=MESH,
    )
    copy.start()
    copy.wait()
    own[...] = acc[pl.ds(pl.multiple_of(me_y * half, 8), half), :] + halves[0]

    copy = pltpu.make_async_remote_copy(
        src_ref=own,
        dst_ref=halves.at[1],
        send_sem=y_send.at[1],
        recv_sem=y_recv.at[1],
        device_id=(pair, partner, me_x),
        device_id_type=MESH,
    )
    copy.start()
    copy.wait()
    gathered[me_x, pl.ds(pl.multiple_of(me_y * half, 8), half), :] = own[...]
    gathered[me_x, pl.ds(pl.multiple_of(partner * half, 8), half), :] = halves[1]

    copies = []
    for by in range(1, inner):
        copy = pltpu.make_async_remote_copy(
            src_ref=gathered.at[me_x],
            dst_ref=gathered.at[me_x],
            send_sem=ag_send.at[by - 1],
            recv_sem=ag_recv.at[by - 1],
            device_id=(pair, me_y, (me_x + by) % inner),
            device_id_type=MESH,
        )
        copy.start()
        copies.append(copy)
    for copy in copies:
        copy.wait()
    for k in range(inner):
        out[pl.ds(k * chunk, chunk), :] = gathered[k]


def rows_sum(v, outer, inner):
    rows, width = v.shape
    chunk = rows // inner
    half = chunk // outer
    return pl.pallas_call(
        functools.partial(rows_sum_kernel, outer, inner),
        out_shape=jax.ShapeDtypeStruct(v.shape, v.dtype),
        in_specs=[pl.BlockSpec(memory_space=pltpu.VMEM)],
        out_specs=pl.BlockSpec(memory_space=pltpu.VMEM),
        scratch_shapes=[
            pltpu.VMEM((inner - 1, chunk, width), jnp.float32),
            pltpu.VMEM((chunk, width), jnp.float32),
            pltpu.VMEM((2, half, width), jnp.float32),
            pltpu.VMEM((half, width), jnp.float32),
            pltpu.VMEM((inner, chunk, width), jnp.float32),
            pltpu.SemaphoreType.DMA((inner - 1,)),
            pltpu.SemaphoreType.DMA((inner - 1,)),
            pltpu.SemaphoreType.DMA((2,)),
            pltpu.SemaphoreType.DMA((2,)),
            pltpu.SemaphoreType.DMA((inner - 1,)),
            pltpu.SemaphoreType.DMA((inner - 1,)),
        ],
        compiler_params=pltpu.CompilerParams(collective_id=0, has_side_effects=True),
    )(v)


def summed_gram(upper, lower, outer, inner):
    width = upper.shape[1]
    row = lax.broadcasted_iota(jnp.int32, (width, width), 0)
    col = lax.broadcasted_iota(jnp.int32, (width, width), 1)
    upper_gram = inner_gram(upper, upper)
    lower_gram = inner_gram(lower, lower)
    cross_gram = inner_gram(upper, lower)
    packed = jnp.where(col >= row, upper_gram, lower_gram)
    tail = jnp.zeros((64, width), jnp.float32).at[0].set(masked_diagonal(lower_gram))
    total = rows_sum(jnp.concatenate([packed, cross_gram, tail]), outer, inner)
    packed, cross_gram, lower_diagonal = total[:width], total[width : 2 * width], total[2 * width]
    strict_upper = jnp.where(col > row, packed, 0.0)
    upper_gram = jnp.where(col >= row, packed, 0.0) + strict_upper.T
    strict_lower = jnp.where(col < row, packed, 0.0)
    lower_gram = strict_lower + strict_lower.T + jnp.where(col == row, lower_diagonal[None, :], 0.0)
    return upper_gram, lower_gram, cross_gram, masked_diagonal(packed), lower_diagonal


def from_behind(x, axis, by):
    count = lax.axis_size(axis)
    pairs = [(i, i + by) for i in range(count) if 0 <= i + by < count]
    return lax.ppermute(x, axis, pairs)


def inner_gram(left, right):
    return lax.dot_general(
        left, right, (((0,), (0,)), ((), ())), precision=high, preferred_element_type=jnp.float32
    )


def masked_diagonal(block):
    width = block.shape[0]
    eye = lax.broadcasted_iota(jnp.int32, (width, width), 0) == lax.broadcasted_iota(jnp.int32, (width, width), 1)
    return jnp.sum(jnp.where(eye, block, 0.0), axis=0)


def normalize(gram, diagonal):
    width = gram.shape[0]
    diagonal = diagonal + epsilon
    inverse = 1.0 / jnp.sqrt(diagonal)
    normed = gram * inverse[:, None] * inverse[None, :]
    spread = 1.5 * jnp.sqrt(jnp.sum(normed * normed)) / jnp.sqrt(jnp.float32(width))
    scaled_gram = normed / spread
    identity = jnp.eye(width, dtype=jnp.float32)
    first_iter = 0.5 * (3.0 * identity - scaled_gram)
    factor = 0.5 * jnp.sqrt(diagonal) / jnp.sqrt(spread)
    return (scaled_gram, first_iter, inverse, factor, identity)


def per_device(matrix, plan, outer, inner):
    local_rows = matrix.shape[0]
    blocks = matrix.reshape(local_rows, -1, BLK)
    slots = jnp.take(blocks, plan, axis=1).reshape(local_rows, -1)
    current = lax.all_to_all(slots, "pair", split_axis=1, concat_axis=0, tiled=True)
    pair_index = lax.axis_index("pair")
    pair_count = lax.axis_size("pair")
    for turn_index in range(STEPS):
        upper = current[:, :BLK]
        lower = current[:, BLK:]
        upper_gram, lower_gram, cross_gram, upper_diagonal, lower_diagonal = summed_gram(
            upper, lower, outer, inner
        )
        gram = jnp.concatenate(
            [
                jnp.concatenate([upper_gram, cross_gram], axis=1),
                jnp.concatenate([cross_gram.T, lower_gram], axis=1),
            ],
            axis=0,
        )
        diagonal = jnp.concatenate([upper_diagonal, lower_diagonal])
        scaled_gram, first_iter, inverse, factor, identity = normalize(gram, diagonal)
        weighted = current * inverse[None, :]
        second_term = jnp.dot(
            scaled_gram, first_iter, precision=fast, preferred_element_type=jnp.float32
        )
        middle = 3.0 * identity - jnp.dot(
            first_iter, second_term, precision=fast, preferred_element_type=jnp.float32
        )
        product = jnp.dot(weighted, middle, precision=fast, preferred_element_type=jnp.float32)
        current = (
            jnp.dot(product, first_iter, precision=fast, preferred_element_type=jnp.float32)
            * factor[None, :]
        )
        upper = current[:, :BLK]
        lower = current[:, BLK:]
        outgoing = jnp.where(pair_index == 0, lower, upper)
        arrived_up = from_behind(outgoing, "pair", 1)
        arrived_down = from_behind(lower, "pair", -1)
        new_upper = jnp.where(pair_index == 0, upper, arrived_up)
        new_lower = jnp.where(pair_index == pair_count - 1, upper, arrived_down)
        current = jnp.concatenate([new_upper, new_lower], axis=1)
    return current


def solution(mesh):
    pairs, rows = mesh.shape["pair"], mesh.shape["rows"]
    inner = 4
    outer = rows // inner
    split = jax.sharding.Mesh(mesh.devices.reshape(pairs, outer, inner), ("pair", "ylo", "x"))
    placed = (P(("ylo", "x", "pair"), None), P())
    return jax.shard_map(
        functools.partial(per_device, outer=outer, inner=inner),
        mesh=split,
        in_specs=placed,
        out_specs=P(("ylo", "x"), "pair"),
        check_vma=False,
    )
```

profile of v0, /device:TPU:97, one launch (start us, length us, event | category | flops | bytes accessed | tf_op | source)
XLA Modules:
  0.0 345.2 jit_solution(3142238716869789443)
XLA Ops:
  1.3 1.8 copy.74
  3.2 2.0 gather_fusion
  5.2 4.1 %copy.46 = f32[32,32,512]{2,1,0:T(8,128)} copy(f32[32,32,512]{2,0,1:T(8,128)} %bitcast.44) | data formatting | bytes 4194304 | tf_op jit(solution)/shard_map/jit(_take)/gather | solution.py:201
  9.3 1.9 gather.7
  11.7 2.5 copy.47
  14.2 7.7 %all-to-all-start = ((f32[32,16,1024]{2,0,1:T(8,128)}), f32[32,16,1024]{2,0,1:T(8,128)S(1)}, u32[]{:S(2)}, u32[]{:S(2)}) async-start(f32[32,16,1024]{2,0,1:T(8,128)} %copy.47), calls=%async_computation | async-start | bytes 4194304 | tf_op jit(solution)/shard_map/all_to_all | solution.py:202
  21.9 29.3 %all-to-all-done = f32[32,16,1024]{2,0,1:T(8,128)S(1)} async-done(((f32[32,16,1024]{2,0,1:T(8,128)}), f32[32,16,1024]{2,0,1:T(8,128)S(1)}, u32[]{:S(2)}, u32[]{:S(2)}) %all-to-all-start) | async-done | bytes 2097184 | tf_op jit(solution)/shard_map/all_to_all | solution.py:202
  51.2 1.9 select_reduce_fusion.3
  53.1 1.9 fusion.53
  55.0 1.9 convolution_select_fusion.1
  56.8 1.5 select_maximum_fusion.1.payload
  58.4 70.2 %shard_map.28 = f32[1088,512]{1,0:T(8,128)} custom-call(f32[1088,512]{1,0:T(8,128)} %select_maximum_fusion.1.payload), custom_call_target="tpu_custom_call" | custom-call | tf_op jit(solution)/shard_map/pallas_call | solution.py:127
  130.6 1.3 copy.48
  131.9 3.9 %bitcast_add_fusion.3 = (f32[512,512]{1,0:T(8,128)}, f32[512]{0:T(512)S(1)}, f32[512,512]{1,0:T(8,128)S(1)}, f32[512,512]{0,1:T(8,128)}, f32[512,512]{1,0:T(8,128)}) fusion(f32[512,512]{0,1:T(8,128)} %copy.48, f32[1088,512]{1,0:T(8,128)} %shard_map.28), kind=kLoop, calls=%fused_computation.64 | loop fusion | flops 2620928 | bytes 7342080 | tf_op jit(solution)/shard_map/add | solution.py:161
  135.8 1.3 copy.50
  137.1 2.7 fusion.50
  139.8 1.6 copy.51
  141.3 3.7 %multiply_reduce_fusion.1 = f32[]{:T(128)} fusion(f32[1024]{0:T(1024)S(1)} %fusion.60, f32[512,512]{1,0:T(8,128)} %fusion.50, f32[512,512]{1,0:T(8,128)S(1)} %copy.51, f32[512,512]{1,0:T(8,128)} %get-tuple-element.36, f32[512,512]{1,0:T(8,128)} %get-tuple-element.32), kind=kLoop, calls=%fused_computation.14 | loop fusion | flops 7340031 | bytes 4198404 | tf_op jit(solution)/shard_map/reduce_sum | solution.py:190
  145.8 10.7 %fusion.16 = f32[1024,1024]{1,0:T(8,128)S(1)} fusion(f32[]{:T(128)S(6)} %div.44, f32[1024]{0:T(1024)S(1)} %fusion.60, f32[512,512]{1,0:T(8,128)} %fusion.50, f32[512,512]{1,0:T(8,128)S(1)} %copy.51, f32[512,512]{1,0:T(8,128)} %get-tuple-element.36, f32[512,512]{1,0:T(8,128)} %get-tuple-element.32), kind=kOutput, calls=%fused_computation.21 | convolution fusion | flops 6459228160 | bytes 8392708 | tf_op jit(solution)/shard_map/dot_general | solution.py:221
  156.6 7.2 %fusion.14 = f32[1024,1024]{1,0:T(8,128)S(1)} fusion(f32[1024,1024]{1,0:T(8,128)S(1)} %fusion.16, f32[]{:T(128)S(6)} %div.44, f32[1024]{0:T(1024)S(1)} %fusion.60, f32[512,512]{1,0:T(8,128)S(1)} %copy-done.5, f32[512,512]{1,0:T(8,128)S(1)} %copy.51, f32[512,512]{1,0:T(8,128)S(1)} %copy-done.4, f32[512,512]{1,0:T(8,128)S(1)} %copy-done.3), kind=kOutput, calls=%fused_computation.20 | convolution fusion | flops 6452936704 | bytes 12587012 | tf_op jit(solution)/shard_map/dot_general | solution.py:224
  163.8 3.9 %fusion.1 = f32[512,1024]{1,0:T(8,128)S(1)} fusion(f32[1024,1024]{1,0:T(8,128)S(1)} %fusion.14, f32[512,1024]{1,0:T(8,128)S(1)} %bitcast.42, f32[1024]{0:T(1024)S(1)} %fusion.60), kind=kOutput, calls=%fused_computation.6 | convolution fusion | flops 3224895488 | bytes 8392704 | tf_op jit(solution)/shard_map/dot_general | solution.py:227
  167.7 4.0 %fusion.43 = f32[512,1024]{1,0:T(8,128)S(1)} fusion(f32[512,1024]{1,0:T(8,128)S(1)} %fusion.1, f32[1024]{0:T(1024)S(1)} %multiply_divide_fusion.1, f32[]{:T(128)S(6)} %div.44, f32[1024]{0:T(1024)S(1)} %fusion.60, f32[512,512]{1,0:T(8,128)S(1)} %copy-done.5, f32[512,512]{1,0:T(8,128)S(1)} %copy.51, f32[512,512]{1,0:T(8,128)S(1)} %copy-done.4, ...), kind=kOutput, calls=%fused_computation.55 | convolution fusion | flops 3232235520 | bytes 8396804 | tf_op jit(solution)/shard_map/dot_general | solution.py:229
  171.7 1.3 copy-done.1
  173.2 4.6 %collective-permute-start = (f32[512,512]{1,0:T(8,128)S(1)}, f32[512,512]{1,0:T(8,128)}, u32[]{:S(2)}, u32[]{:S(2)}) collective-permute-start(f32[512,512]{1,0:T(8,128)S(1)} %get-tuple-element.43), channel_id=1, source_target_pairs={{0,8},{8,16},{16,24},{24,32},{32,40},{40,48},{48,56},{56,64},{64,7... | collective-permute-start | bytes 3145736 | tf_op jit(solution)/shard_map/ppermute | solution.py:170
  177.8 2.5 collective-permute-start.1
  180.8 8.7 %collective-permute-done = f32[512,512]{1,0:T(8,128)} collective-permute-done((f32[512,512]{1,0:T(8,128)S(1)}, f32[512,512]{1,0:T(8,128)}, u32[]{:S(2)}, u32[]{:S(2)}) %collective-permute-start) | collective-permute-done | bytes 1048608 | tf_op jit(solution)/shard_map/ppermute | solution.py:170
  189.5 8.1 %collective-permute-done.1 = f32[512,512]{1,0:T(8,128)} collective-permute-done((f32[512,512]{1,0:T(8,128)S(1)}, f32[512,512]{1,0:T(8,128)}, u32[]{:S(2)}, u32[]{:S(2)}) %collective-permute-start.1) | collective-permute-done | bytes 1048608 | tf_op jit(solution)/shard_map/ppermute | solution.py:170
  197.6 2.2 slice_select_fusion.4
  199.9 1.9 select_reduce_fusion.1
  201.7 1.9 fusion.84
  203.6 1.9 convolution_select_fusion
  205.5 1.5 select_maximum_fusion.payload
  207.0 68.7 %shard_map.29 = f32[1088,512]{1,0:T(8,128)} custom-call(f32[1088,512]{1,0:T(8,128)} %select_maximum_fusion.payload), custom_call_target="tpu_custom_call" | custom-call | tf_op jit(solution)/shard_map/pallas_call | solution.py:127
  275.7 2.3 slice.71
  278.6 1.6 copy.61
  281.5 2.6 copy.60
  284.1 4.4 %bitcast_add_fusion.1 = (f32[512,512]{1,0:T(8,128)}, f32[512]{0:T(512)S(1)}, f32[512,512]{1,0:T(8,128)S(1)}, f32[512,512]{1,0:T(8,128)}) fusion(f32[512,512]{0,1:T(8,128)} %copy-done, f32[1088,512]{1,0:T(8,128)} %shard_map.29, f32[512]{0:T(512)S(1)} %bitcast.55, f32[512,512]{1,0:T(8,128)} %copy.60, f32[512,512]{0,1:T(8,128)} %broadcast_select_fusion.1), kind=kLoop, calls=%fused_computation.61 | loop fusion | flops 3145216 | bytes 8392704 | tf_op jit(solution)/shard_map/add | solution.py:161
  288.4 1.3 copy.62
  289.7 3.8 %multiply_reduce_fusion = f32[]{:T(128)} fusion(f32[1024]{0:T(1024)S(1)} %fusion.59, f32[512,512]{1,0:T(8,128)} %get-tuple-element.49, f32[512,512]{1,0:T(8,128)} %bitcast.45, f32[512,512]{1,0:T(8,128)S(1)} %get-tuple-element.31, f32[512,512]{1,0:T(8,128)} %get-tuple-element.29), kind=kLoop, calls=%fused_computation.13 | loop fusion | flops 7340031 | bytes 4198404 | tf_op jit(solution)/shard_map/reduce_sum | solution.py:190
  294.3 10.5 %fusion.10 = f32[1024,1024]{1,0:T(8,128)S(1)} fusion(f32[]{:T(128)S(6)} %div.49, f32[1024]{0:T(1024)S(1)} %fusion.59, f32[512,512]{1,0:T(8,128)} %get-tuple-element.49, f32[512,512]{1,0:T(8,128)} %bitcast.46, f32[512,512]{1,0:T(8,128)S(1)} %get-tuple-element.31, f32[512,512]{1,0:T(8,128)} %get-tuple-element.29), kind=kOutput, calls=%fused_computation.18 | convolution fusion | flops 6459228160 | bytes 8392708 | tf_op jit(solution)/shard_map/dot_general | solution.py:221
  304.9 7.2 %fusion.8 = f32[1024,1024]{1,0:T(8,128)S(1)} fusion(f32[1024,1024]{1,0:T(8,128)S(1)} %fusion.10, f32[]{:T(128)S(6)} %div.49, f32[1024]{0:T(1024)S(1)} %fusion.59, f32[512,512]{1,0:T(8,128)S(1)} %copy-done.7, f32[512,512]{1,0:T(8,128)S(1)} %bitcast.47, f32[512,512]{1,0:T(8,128)S(1)} %get-tuple-element.31, f32[512,512]{1,0:T(8,128)S(1)} %copy-done.6), kind=kOutput, calls=%fused_computation.17 | convolution fusion | flops 6452936704 | bytes 12587012 | tf_op jit(solution)/shard_map/dot_general | solution.py:224
  312.1 3.9 %fusion.3 = f32[512,1024]{1,0:T(8,128)S(1)} fusion(f32[1024,1024]{1,0:T(8,128)S(1)} %fusion.8, f32[512,512]{1,0:T(8,128)S(1)} %get-tuple-element.42, f32[512,512]{1,0:T(8,128)S(1)} %get-tuple-element.41, f32[1024]{0:T(1024)S(1)} %fusion.59), kind=kOutput, calls=%fused_computation.8 | convolution fusion | flops 3225419776 | bytes 8392704 | tf_op jit(solution)/shard_map/dot_general | solution.py:227
  316.0 4.0 %fusion.46 = f32[512,1024]{1,0:T(8,128)S(1)} fusion(f32[512,1024]{1,0:T(8,128)S(1)} %fusion.3, f32[1024]{0:T(1024)S(1)} %multiply_divide_fusion, f32[]{:T(128)S(6)} %div.49, f32[1024]{0:T(1024)S(1)} %fusion.59, f32[512,512]{1,0:T(8,128)S(1)} %copy-done.7, f32[512,512]{1,0:T(8,128)S(1)} %bitcast.48, f32[512,512]{1,0:T(8,128)S(1)} %get-tuple-element.31, ...), kind=kOutput, calls=%fused_computation.56 | convolution fusion | flops 3232235520 | bytes 8396804 | tf_op jit(solution)/shard_map/dot_general | solution.py:229
  320.2 3.0 collective-permute-start.2
  323.3 1.9 collective-permute-start.3
  325.2 9.8 %collective-permute-done.2 = f32[512,512]{1,0:T(8,128)S(1)} collective-permute-done((f32[512,512]{1,0:T(8,128)S(1)}, f32[512,512]{1,0:T(8,128)S(1)}, u32[]{:S(2)}, u32[]{:S(2)}) %collective-permute-start.2) | collective-permute-done | bytes 1048608 | tf_op jit(solution)/shard_map/ppermute | solution.py:170
  335.0 8.0 %collective-permute-done.3 = f32[512,512]{1,0:T(8,128)S(1)} collective-permute-done((f32[512,512]{1,0:T(8,128)S(1)}, f32[512,512]{1,0:T(8,128)S(1)}, u32[]{:S(2)}, u32[]{:S(2)}) %collective-permute-start.3) | collective-permute-done | bytes 1048608 | tf_op jit(solution)/shard_map/ppermute | solution.py:170
  343.3 1.5 pad_maximum_fusion
  (35 shorter events, 7.2 us)
Async XLA Ops:
  14.2 37.0 %all-to-all-start = ((f32[32,16,1024]{2,0,1:T(8,128)}), f32[32,16,1024]{2,0,1:T(8,128)S(1)}, u32[]{:S(2)}, u32[]{:S(2)}) async-start(f32[32,16,1024]{2,0,1:T(8,128)} %copy.47), calls=%async_computation | async-start | bytes 4194304 | tf_op jit(solution)/shard_map/all_to_all | solution.py:202
  145.8 10.8 %copy-start.3 = (f32[512,512]{1,0:T(8,128)S(1)}, f32[512,512]{1,0:T(8,128)}, u32[]{:S(2)}) copy-start(f32[512,512]{1,0:T(8,128)} %get-tuple-element.32) | copy-start | bytes 3145732
  145.8 10.8 %copy-start.4 = (f32[512,512]{1,0:T(8,128)S(1)}, f32[512,512]{1,0:T(8,128)}, u32[]{:S(2)}) copy-start(f32[512,512]{1,0:T(8,128)} %get-tuple-element.36) | copy-start | bytes 3145732
  145.8 10.8 %copy-start.5 = (f32[512,512]{1,0:T(8,128)S(1)}, f32[512,512]{1,0:T(8,128)}, u32[]{:S(2)}) copy-start(f32[512,512]{1,0:T(8,128)} %fusion.50) | copy-start | bytes 3145732
  171.6 1.3 copy-start.1
  173.2 16.3 %collective-permute-start = (f32[512,512]{1,0:T(8,128)S(1)}, f32[512,512]{1,0:T(8,128)}, u32[]{:S(2)}, u32[]{:S(2)}) collective-permute-start(f32[512,512]{1,0:T(8,128)S(1)} %get-tuple-element.43), channel_id=1, source_target_pairs={{0,8},{8,16},{16,24},{24,32},{32,40},{40,48},{48,56},{56,64},{64,7... | collective-permute-start | bytes 3145736 | tf_op jit(solution)/shard_map/ppermute | solution.py:170
  177.8 19.8 %collective-permute-start.1 = (f32[512,512]{1,0:T(8,128)S(1)}, f32[512,512]{1,0:T(8,128)}, u32[]{:S(2)}, u32[]{:S(2)}) collective-permute-start(f32[512,512]{1,0:T(8,128)S(1)} %get-tuple-element.44), channel_id=1, source_target_pairs={{8,0},{16,8},{24,16},{32,24},{40,32},{48,40},{56,48},{64,56},{72,6... | collective-permute-start | bytes 3145736 | tf_op jit(solution)/shard_map/ppermute | solution.py:170
  280.2 3.9 %copy-start = (f32[512,512]{0,1:T(8,128)}, f32[512,512]{0,1:T(8,128)S(1)}, u32[]{:S(2)}) copy-start(f32[512,512]{0,1:T(8,128)S(1)} %copy.61) | copy-start | bytes 3145732
  294.3 10.6 %copy-start.2 = (f32[512,512]{0,1:T(8,128)S(1)}, f32[512,512]{0,1:T(8,128)}, u32[]{:S(2)}) copy-start(f32[512,512]{0,1:T(8,128)} %copy.62) | copy-start | bytes 3145732
  294.3 10.6 %copy-start.6 = (f32[512,512]{1,0:T(8,128)S(1)}, f32[512,512]{1,0:T(8,128)}, u32[]{:S(2)}) copy-start(f32[512,512]{1,0:T(8,128)} %get-tuple-element.29) | copy-start | bytes 3145732
  294.3 10.6 %copy-start.7 = (f32[512,512]{1,0:T(8,128)S(1)}, f32[512,512]{1,0:T(8,128)}, u32[]{:S(2)}) copy-start(f32[512,512]{1,0:T(8,128)} %get-tuple-element.49) | copy-start | bytes 3145732
  320.2 14.7 %collective-permute-start.2 = (f32[512,512]{1,0:T(8,128)S(1)}, f32[512,512]{1,0:T(8,128)S(1)}, u32[]{:S(2)}, u32[]{:S(2)}) collective-permute-start(f32[512,512]{1,0:T(8,128)S(1)} %get-tuple-element.39), channel_id=1, source_target_pairs={{0,8},{8,16},{16,24},{24,32},{32,40},{40,48},{48,56},{56,64},{64,7... | collective-permute-start | bytes 3145736 | tf_op jit(solution)/shard_map/ppermute | solution.py:170
  323.3 19.7 %collective-permute-start.3 = (f32[512,512]{1,0:T(8,128)S(1)}, f32[512,512]{1,0:T(8,128)S(1)}, u32[]{:S(2)}, u32[]{:S(2)}) collective-permute-start(f32[512,512]{1,0:T(8,128)S(1)} %get-tuple-element.40), channel_id=1, source_target_pairs={{8,0},{16,8},{24,16},{32,24},{40,32},{48,40},{56,48},{64,56},{72,6... | collective-permute-start | bytes 3145736 | tf_op jit(solution)/shard_map/ppermute | solution.py:170
where the time goes:
time: 349 us; the launch traced here: 345 us
  Pallas kernels  139 us (40%)
  waiting for transfers between devices  63.9 us (18%)
  matrix products  62.5 us (18%)
  other arithmetic  28.9 us (8%)
  local copies, waits for them, and re-layouts  28.9 us (8%)
  starting transfers between devices  19.7 us (6%)
    pallas_call x2, Pallas kernels, rows_sum(): pl.pallas_call(functools.partial(rows_sum_kernel, outer, inner), out_shap...  139 us
    ppermute x4, waiting for transfers between devices, from_behind(): return lax.ppermute(x, axis, pairs)  34.6 us
    all_to_all x1, waiting for transfers between devices, per_device(): lax.all_to_all(slots, 'pair', split_axis=1, concat_axis=0, tiled=True)  29.3 us
    dot_general x2, matrix products, per_device(): jnp.dot(scaled_gram, first_iter, precision=fast, preferred_element_type=j...  21.2 us
    dot_general x2, matrix products, per_device(): jnp.dot(first_iter, second_term, precision=fast, preferred_element_type=j...  14.4 us
    ppermute x4, starting transfers between devices, from_behind(): return lax.ppermute(x, axis, pairs)  12 us
    dot_general x6, matrix products, inner_gram(): lax.dot_general(left, right, (((0,), (0,)), ((), ())), precision=high, pr...  11.2 us
    add x2, other arithmetic, summed_gram(): upper_gram = jnp.where(col >= row, packed, 0.0) + strict_upper.T  8.25 us
  transfers between devices with their start and end apart: 5, of which 5 were waited for; matrix products, arithmetic and copies ran while one was open for 0% of the time, Pallas kernels for 0%

commit v1 on v0

--- a/solution.py
+++ b/solution.py
@@ -172,7 +172,7 @@
 
 def inner_gram(left, right):
     return lax.dot_general(
-        left, right, (((0,), (0,)), ((), ())), precision=high, preferred_element_type=jnp.float32
+        left, right, (((0,), (0,)), ((), ())), precision=fast, preferred_element_type=jnp.float32
     )
 
 
@@ -218,17 +218,11 @@
         diagonal = jnp.concatenate([upper_diagonal, lower_diagonal])
         scaled_gram, first_iter, inverse, factor, identity = normalize(gram, diagonal)
         weighted = current * inverse[None, :]
-        second_term = jnp.dot(
-            scaled_gram, first_iter, precision=fast, preferred_element_type=jnp.float32
-        )
-        middle = 3.0 * identity - jnp.dot(
-            first_iter, second_term, precision=fast, preferred_element_type=jnp.float32
-        )
-        product = jnp.dot(weighted, middle, precision=fast, preferred_element_type=jnp.float32)
-        current = (
-            jnp.dot(product, first_iter, precision=fast, preferred_element_type=jnp.float32)
-            * factor[None, :]
-        )
+        applied = jnp.dot(weighted, first_iter, precision=fast, preferred_element_type=jnp.float32)
+        chain = jnp.dot(applied, scaled_gram, precision=fast, preferred_element_type=jnp.float32)
+        chain = jnp.dot(chain, first_iter, precision=fast, preferred_element_type=jnp.float32)
+        chain = jnp.dot(chain, first_iter, precision=fast, preferred_element_type=jnp.float32)
+        current = (3.0 * applied - chain) * factor[None, :]
         upper = current[:, :BLK]
         lower = current[:, BLK:]
         outgoing = jnp.where(pair_index == 0, lower, upper)

time: 349 us -> 327 us (0.937)
  matrix products: 62.5 us -> 35.4 us
  other arithmetic: 28.9 us -> 33.7 us
    dot_general x14, matrix products: 62.5 us -> 35.4 us  [the longest x4 14.1 us: per_device(): jnp.dot(chain, first_iter, precision=fast, preferred_element_type=jnp.flo...]
    div x0 -> x2, other arithmetic: none -> 4.8 us  [normalize(): scaled_gram = normed / spread]
where the time goes in v1:
time: 327 us; the launch traced here: 323 us
  Pallas kernels  139 us (43%)
  waiting for transfers between devices  63.6 us (19%)
  matrix products  35.4 us (11%)
  other arithmetic  33.7 us (10%)
  local copies, waits for them, and re-layouts  29 us (9%)
  starting transfers between devices  20 us (6%)
    pallas_call x2, Pallas kernels, rows_sum(): pl.pallas_call(functools.partial(rows_sum_kernel, outer, inner), out_shap...  139 us
    ppermute x4, waiting for transfers between devices, from_behind(): return lax.ppermute(x, axis, pairs)  34.2 us
    all_to_all x1, waiting for transfers between devices, per_device(): lax.all_to_all(slots, 'pair', split_axis=1, concat_axis=0, tiled=True)  29.3 us
    dot_general x4, matrix products, per_device(): jnp.dot(chain, first_iter, precision=fast, preferred_element_type=jnp.flo...  14.1 us
    ppermute x4, starting transfers between devices, from_behind(): return lax.ppermute(x, axis, pairs)  12.4 us
    add x2, other arithmetic, summed_gram(): upper_gram = jnp.where(col >= row, packed, 0.0) + strict_upper.T  8.24 us
    gather x3, local copies, waits for them, and re-layouts, per_device(): slots = jnp.take(blocks, plan, axis=1).reshape(local_rows, -1)  8.09 us
    dot_general x2, matrix products, per_device(): jnp.dot(applied, scaled_gram, precision=fast, preferred_element_type=jnp....  7.95 us
  transfers between devices with their start and end apart: 5, of which 5 were waited for; matrix products, arithmetic and copies ran while one was open for 0% of the time, Pallas kernels for 0%

profile of v1, /device:TPU:97, one launch (start us, length us, event | category | flops | bytes accessed | tf_op | source)
XLA Modules:
  0.0 322.5 jit_solution(10498307305533369563)
XLA Ops:
  1.3 1.8 copy.74
  3.2 2.0 gather_fusion
  5.2 4.2 %copy.46 = f32[32,32,512]{2,1,0:T(8,128)} copy(f32[32,32,512]{2,0,1:T(8,128)} %bitcast.50) | data formatting | bytes 4194304 | tf_op jit(solution)/shard_map/jit(_take)/gather | solution.py:201
  9.3 1.9 gather.7
  11.7 2.5 copy.47
  14.3 7.6 %all-to-all-start = ((f32[32,16,1024]{2,0,1:T(8,128)}), f32[32,16,1024]{2,0,1:T(8,128)S(1)}, u32[]{:S(2)}, u32[]{:S(2)}) async-start(f32[32,16,1024]{2,0,1:T(8,128)} %copy.47), calls=%async_computation | async-start | bytes 4194304 | tf_op jit(solution)/shard_map/all_to_all | solution.py:202
  21.9 29.3 %all-to-all-done = f32[32,16,1024]{2,0,1:T(8,128)S(1)} async-done(((f32[32,16,1024]{2,0,1:T(8,128)}), f32[32,16,1024]{2,0,1:T(8,128)S(1)}, u32[]{:S(2)}, u32[]{:S(2)}) %all-to-all-start) | async-done | bytes 2097184 | tf_op jit(solution)/shard_map/all_to_all | solution.py:202
  51.2 1.0 select_reduce_fusion.3
  54.4 1.5 select_maximum_fusion.1.payload
  55.9 70.2 %shard_map.28 = f32[1088,512]{1,0:T(8,128)} custom-call(f32[1088,512]{1,0:T(8,128)} %select_maximum_fusion.1.payload), custom_call_target="tpu_custom_call" | custom-call | tf_op jit(solution)/shard_map/pallas_call | solution.py:127
  126.2 1.3 slice.66
  128.2 1.3 copy.48
  129.5 3.9 %bitcast_add_fusion.3 = (f32[512,512]{1,0:T(8,128)}, f32[512]{0:T(512)S(1)}, f32[512,512]{1,0:T(8,128)S(1)}, f32[512,512]{0,1:T(8,128)}, f32[512,512]{1,0:T(8,128)}) fusion(f32[512,512]{0,1:T(8,128)} %copy.48, f32[1088,512]{1,0:T(8,128)} %shard_map.28), kind=kLoop, calls=%fused_computation.56 | loop fusion | flops 2620928 | bytes 7342080 | tf_op jit(solution)/shard_map/add | solution.py:161
  133.4 1.3 copy.50
  134.7 2.7 fusion.42
  137.4 1.6 copy.51
  138.9 3.7 %multiply_reduce_fusion.1 = f32[]{:T(128)} fusion(f32[1024]{0:T(1024)S(1)} %fusion.52, f32[512,512]{1,0:T(8,128)} %fusion.42, f32[512,512]{1,0:T(8,128)S(1)} %copy.51, f32[512,512]{1,0:T(8,128)} %get-tuple-element.36, f32[512,512]{1,0:T(8,128)} %get-tuple-element.32), kind=kLoop, calls=%fused_computation.10 | loop fusion | flops 7340031 | bytes 4198404 | tf_op jit(solution)/shard_map/reduce_sum | solution.py:190
  143.3 2.4 broadcast_divide_fusion.1
  145.7 3.5 %fusion.14 = f32[512,1024]{1,0:T(8,128)S(1)} fusion(f32[1024,1024]{1,0:T(8,128)S(1)} %broadcast_divide_fusion.1, f32[512,1024]{1,0:T(8,128)S(1)} %bitcast.46, f32[1024]{0:T(1024)S(1)} %fusion.52), kind=kOutput, calls=%fused_computation.20 | convolution fusion | flops 3225944064 | bytes 8392704 | tf_op jit(solution)/shard_map/dot_general | solution.py:221
  149.2 4.0 %fusion.72 = f32[512,1024]{1,0:T(8,128)S(1)} fusion(f32[512,1024]{1,0:T(8,128)S(1)} %fusion.14, f32[1024,1024]{1,0:T(8,128)S(1)} %broadcast_divide_fusion.1), kind=kOutput, calls=%fused_computation.112 | convolution fusion | flops 3221225472 | bytes 8388608 | tf_op jit(solution)/shard_map/dot_general | solution.py:222
  153.2 3.5 %fusion.12 = f32[512,1024]{1,0:T(8,128)S(1)} fusion(f32[512,1024]{1,0:T(8,128)S(1)} %fusion.72, f32[1024,1024]{1,0:T(8,128)S(1)} %broadcast_divide_fusion.1), kind=kOutput, calls=%fused_computation.19 | convolution fusion | flops 3225419776 | bytes 8388608 | tf_op jit(solution)/shard_map/dot_general | solution.py:223
  156.8 3.6 %subtract_multiply_fusion.1 = f32[512,1024]{1,0:T(8,128)S(1)} fusion(f32[512,1024]{1,0:T(8,128)S(1)} %fusion.14, f32[512,1024]{1,0:T(8,128)S(1)} %fusion.12, f32[1024,1024]{1,0:T(8,128)S(1)} %broadcast_divide_fusion.1, f32[1024]{0:T(1024)S(1)} %multiply_divide_fusion.1), kind=kOutput, calls=%fused_computation.28 | convolution fusion | flops 3226992640 | bytes 10489856 | tf_op jit(solution)/shard_map/dot_general | solution.py:224
  160.3 1.3 copy-done
  161.9 4.6 %collective-permute-start = (f32[512,512]{1,0:T(8,128)S(1)}, f32[512,512]{1,0:T(8,128)}, u32[]{:S(2)}, u32[]{:S(2)}) collective-permute-start(f32[512,512]{1,0:T(8,128)S(1)} %get-tuple-element.43), channel_id=1, source_target_pairs={{0,8},{8,16},{16,24},{24,32},{32,40},{40,48},{48,56},{56,64},{64,7... | collective-permute-start | bytes 3145736 | tf_op jit(solution)/shard_map/ppermute | solution.py:170
  166.5 2.9 collective-permute-start.1
  169.9 8.3 %collective-permute-done = f32[512,512]{1,0:T(8,128)} collective-permute-done((f32[512,512]{1,0:T(8,128)S(1)}, f32[512,512]{1,0:T(8,128)}, u32[]{:S(2)}, u32[]{:S(2)}) %collective-permute-start) | collective-permute-done | bytes 1048608 | tf_op jit(solution)/shard_map/ppermute | solution.py:170
  178.2 8.1 %collective-permute-done.1 = f32[512,512]{1,0:T(8,128)} collective-permute-done((f32[512,512]{1,0:T(8,128)S(1)}, f32[512,512]{1,0:T(8,128)}, u32[]{:S(2)}, u32[]{:S(2)}) %collective-permute-start.1) | collective-permute-done | bytes 1048608 | tf_op jit(solution)/shard_map/ppermute | solution.py:170
  186.3 2.2 slice_select_fusion.4
  188.5 1.0 select_reduce_fusion.1
  191.6 1.5 select_maximum_fusion.payload
  193.2 68.7 %shard_map.29 = f32[1088,512]{1,0:T(8,128)} custom-call(f32[1088,512]{1,0:T(8,128)} %select_maximum_fusion.payload), custom_call_target="tpu_custom_call" | custom-call | tf_op jit(solution)/shard_map/pallas_call | solution.py:127
  261.9 2.3 slice.71
  264.9 1.6 copy.61
  266.4 1.3 broadcast_select_fusion.1
  267.7 2.5 copy.60
  270.3 4.4 %bitcast_add_fusion.1 = (f32[512,512]{1,0:T(8,128)}, f32[512]{0:T(512)S(1)}, f32[512,512]{1,0:T(8,128)S(1)}, f32[512,512]{1,0:T(8,128)}) fusion(f32[512,512]{0,1:T(8,128)} %copy-done.1, f32[1088,512]{1,0:T(8,128)} %shard_map.29, f32[512]{0:T(512)S(1)} %bitcast.57, f32[512,512]{1,0:T(8,128)} %copy.60, f32[512,512]{0,1:T(8,128)} %broadcast_select_fusion.1), kind=kLoop, calls=%fused_computation.53 | loop fusion | flops 3145216 | bytes 8392704 | tf_op jit(solution)/shard_map/add | solution.py:161
  274.6 1.3 copy.62
  276.0 3.8 %multiply_reduce_fusion = f32[]{:T(128)} fusion(f32[1024]{0:T(1024)S(1)} %fusion.51, f32[512,512]{1,0:T(8,128)} %get-tuple-element.49, f32[512,512]{1,0:T(8,128)} %bitcast.47, f32[512,512]{1,0:T(8,128)S(1)} %get-tuple-element.31, f32[512,512]{1,0:T(8,128)} %get-tuple-element.29), kind=kLoop, calls=%fused_computation.9 | loop fusion | flops 7340031 | bytes 4198404 | tf_op jit(solution)/shard_map/reduce_sum | solution.py:190
  280.5 2.4 broadcast_divide_fusion
  282.9 3.5 %fusion.8 = f32[512,1024]{1,0:T(8,128)S(1)} fusion(f32[1024,1024]{1,0:T(8,128)S(1)} %broadcast_divide_fusion, f32[512,512]{1,0:T(8,128)S(1)} %get-tuple-element.42, f32[512,512]{1,0:T(8,128)S(1)} %get-tuple-element.41, f32[1024]{0:T(1024)S(1)} %fusion.51), kind=kOutput, calls=%fused_computation.17 | convolution fusion | flops 3226468352 | bytes 8392704 | tf_op jit(solution)/shard_map/dot_general | solution.py:221
  286.5 4.0 %fusion.74 = f32[512,1024]{1,0:T(8,128)S(1)} fusion(f32[512,1024]{1,0:T(8,128)S(1)} %fusion.8, f32[1024,1024]{1,0:T(8,128)S(1)} %broadcast_divide_fusion), kind=kOutput, calls=%fused_computation.114 | convolution fusion | flops 3221225472 | bytes 8388608 | tf_op jit(solution)/shard_map/dot_general | solution.py:222
  290.4 3.5 %fusion.6 = f32[512,1024]{1,0:T(8,128)S(1)} fusion(f32[512,1024]{1,0:T(8,128)S(1)} %fusion.74, f32[1024,1024]{1,0:T(8,128)S(1)} %broadcast_divide_fusion), kind=kOutput, calls=%fused_computation.16 | convolution fusion | flops 3225419776 | bytes 8388608 | tf_op jit(solution)/shard_map/dot_general | solution.py:223
  294.0 3.6 %subtract_multiply_fusion = f32[512,1024]{1,0:T(8,128)S(1)} fusion(f32[512,1024]{1,0:T(8,128)S(1)} %fusion.8, f32[512,1024]{1,0:T(8,128)S(1)} %fusion.6, f32[1024,1024]{1,0:T(8,128)S(1)} %broadcast_divide_fusion, f32[1024]{0:T(1024)S(1)} %multiply_divide_fusion), kind=kOutput, calls=%fused_computation.26 | convolution fusion | flops 3226992640 | bytes 10489856 | tf_op jit(solution)/shard_map/dot_general | solution.py:224
  297.8 3.0 collective-permute-start.2
  300.8 1.9 collective-permute-start.3
  302.7 9.8 %collective-permute-done.2 = f32[512,512]{1,0:T(8,128)S(1)} collective-permute-done((f32[512,512]{1,0:T(8,128)S(1)}, f32[512,512]{1,0:T(8,128)S(1)}, u32[]{:S(2)}, u32[]{:S(2)}) %collective-permute-start.2) | collective-permute-done | bytes 1048608 | tf_op jit(solution)/shard_map/ppermute | solution.py:170
  312.5 8.0 %collective-permute-done.3 = f32[512,512]{1,0:T(8,128)S(1)} collective-permute-done((f32[512,512]{1,0:T(8,128)S(1)}, f32[512,512]{1,0:T(8,128)S(1)}, u32[]{:S(2)}, u32[]{:S(2)}) %collective-permute-start.3) | collective-permute-done | bytes 1048608 | tf_op jit(solution)/shard_map/ppermute | solution.py:170
  320.9 1.5 pad_maximum_fusion
  (25 shorter events, 8.7 us)
Async XLA Ops:
  14.3 37.0 %all-to-all-start = ((f32[32,16,1024]{2,0,1:T(8,128)}), f32[32,16,1024]{2,0,1:T(8,128)S(1)}, u32[]{:S(2)}, u32[]{:S(2)}) async-start(f32[32,16,1024]{2,0,1:T(8,128)} %copy.47), calls=%async_computation | async-start | bytes 4194304 | tf_op jit(solution)/shard_map/all_to_all | solution.py:202
  160.3 1.3 copy-start
  161.9 16.3 %collective-permute-start = (f32[512,512]{1,0:T(8,128)S(1)}, f32[512,512]{1,0:T(8,128)}, u32[]{:S(2)}, u32[]{:S(2)}) collective-permute-start(f32[512,512]{1,0:T(8,128)S(1)} %get-tuple-element.43), channel_id=1, source_target_pairs={{0,8},{8,16},{16,24},{24,32},{32,40},{40,48},{48,56},{56,64},{64,7... | collective-permute-start | bytes 3145736 | tf_op jit(solution)/shard_map/ppermute | solution.py:170
  166.5 19.8 %collective-permute-start.1 = (f32[512,512]{1,0:T(8,128)S(1)}, f32[512,512]{1,0:T(8,128)}, u32[]{:S(2)}, u32[]{:S(2)}) collective-permute-start(f32[512,512]{1,0:T(8,128)S(1)} %get-tuple-element.44), channel_id=1, source_target_pairs={{8,0},{16,8},{24,16},{32,24},{40,32},{48,40},{56,48},{64,56},{72,6... | collective-permute-start | bytes 3145736 | tf_op jit(solution)/shard_map/ppermute | solution.py:170
  266.4 3.8 %copy-start.1 = (f32[512,512]{0,1:T(8,128)}, f32[512,512]{0,1:T(8,128)S(1)}, u32[]{:S(2)}) copy-start(f32[512,512]{0,1:T(8,128)S(1)} %copy.61) | copy-start | bytes 3145732
  297.8 14.7 %collective-permute-start.2 = (f32[512,512]{1,0:T(8,128)S(1)}, f32[512,512]{1,0:T(8,128)S(1)}, u32[]{:S(2)}, u32[]{:S(2)}) collective-permute-start(f32[512,512]{1,0:T(8,128)S(1)} %get-tuple-element.39), channel_id=1, source_target_pairs={{0,8},{8,16},{16,24},{24,32},{32,40},{40,48},{48,56},{56,64},{64,7... | collective-permute-start | bytes 3145736 | tf_op jit(solution)/shard_map/ppermute | solution.py:170
  300.8 19.7 %collective-permute-start.3 = (f32[512,512]{1,0:T(8,128)S(1)}, f32[512,512]{1,0:T(8,128)S(1)}, u32[]{:S(2)}, u32[]{:S(2)}) collective-permute-start(f32[512,512]{1,0:T(8,128)S(1)} %get-tuple-element.40), channel_id=1, source_target_pairs={{8,0},{16,8},{24,16},{32,24},{40,32},{48,40},{56,48},{64,56},{72,6... | collective-permute-start | bytes 3145736 | tf_op jit(solution)/shard_map/ppermute | solution.py:170
